TPU v7x, 256 devices: a whole 4x4x8 slice. The times are simulated.
256 devices in a mesh: dap: 128 (over y, x, z_hi, core), dp: 2 (over z_lo).
Axes of the slice: x: 4, y: 4, z: 8 (z_hi: 4, z_lo: 2; z = z_hi * 2 + z_lo), core: 2. Of those that a mesh axis runs over, the one named last changes fastest.
Arguments:
- pair: bfloat16 [512, 256, 128], P(('dp', 'dap')), parts along dimension 0
- token_mask: int32 [512], P('dp'), parts along dimension 0, may hold values from 0 to 1, as said below
- chain_ids: int32 [512], P('dp'), parts along dimension 0, may hold values from 0 to 3, never falling along the last dimension, each value on 1 to 128 neighbouring positions
- proj_weight: bfloat16 [128, 512], replicated
- bias_weight: bfloat16 [128, 4], replicated, may hold values from -0.5 to 0.5
- chain_weight: float32 [4], replicated, may hold values from -1.5 to 1.5
- out_weight: bfloat16 [128, 128], replicated, may hold values from -0.5 to 0.5
- cotangent: bfloat16 [512, 256, 128], P(('dp', 'dap')), parts along dimension 0, may hold values from -24 to 24
Outputs:
- next_pair_t: float32 [512, 256, 128], P(('dp', 'dap')), parts along dimension 0
- pair_grad: bfloat16 [512, 256, 128], P(('dp', 'dap')), parts along dimension 0
- proj_grad: float32 [256, 512], P('dp'), parts along dimension 0
- bias_weight_grad: float32 [256, 4], P('dp'), parts along dimension 0
- chain_grad: float32 [8], P('dp'), parts along dimension 0
- out_grad: float32 [256, 128], P('dp'), parts along dimension 0
There are 2 independent parts, one for each index of `dp`. A program takes and returns all parts, laid end to end along the dimension named above; an argument that names none is the same for every part. Nothing has to cross between parts.
Inputs may be any that keep to these rules, and one draw needn't show every extreme that they name: `token_mask`: tokens are real up to some point and padding after it; the first 128 tokens are real and the last token is padding. `chain_ids`: chain numbers never fall along the tokens; every chain has 1 to 128 tokens, one chain exactly 128.
All inputs are finite; a program needn't handle non-finite values.
Results may differ from a plain program's by a relative error of at most 0.011.
Values may be sent and summed in bfloat16 or wider, within the bound.
A program may use at most 64 MiB of HBM per device.

v0:
```python
import jax
import jax.numpy as jnp
from jax import lax
from jax.sharding import PartitionSpec as P

H = 4
DH = 32
HD = 128
epsilon = 1e-05
contract_rows = (((0,), (0,)), ((), ()))
contract_cols = (((1,), (1,)), ((), ()))


def normalize(pair):
    values_f = pair.astype(jnp.float32)
    centered = values_f - jnp.mean(values_f, axis=-1, keepdims=True)
    inverse = lax.rsqrt(jnp.mean(centered * centered, axis=-1, keepdims=True) + epsilon)
    return (centered * inverse, inverse)


def row_softmax(query_row, key_row, bias_head, extra_head):
    scores = lax.dot_general(query_row, key_row, contract_cols, preferred_element_type=jnp.float32)
    scores = scores + bias_head.astype(jnp.float32) + extra_head
    highest = jnp.max(scores, axis=1, keepdims=True)
    expo_s = jnp.exp(scores - highest)
    return expo_s / jnp.sum(expo_s, axis=1, keepdims=True)


def forward_rows(query_h, key_h, value_h, bias_head, extra_head):

    def forward_one_row(items):
        query_row, key_row, value_row = items
        attention = row_softmax(query_row, key_row, bias_head, extra_head)
        return jnp.dot(
            attention.astype(jnp.bfloat16), value_row, preferred_element_type=jnp.float32
        )

    return lax.map(forward_one_row, (query_h, key_h, value_h))


def backward_rows(query_h, key_h, value_h, grad_h, bias_head, extra_head):

    def backward_one_row(summed, items):
        query_row, key_row, value_row, grad_row = items
        attention = row_softmax(query_row, key_row, bias_head, extra_head)
        d_probs = lax.dot_general(
            grad_row, value_row, contract_cols, preferred_element_type=jnp.float32
        )
        inner_sum = jnp.sum(attention * d_probs, axis=1, keepdims=True)
        d_scores = attention * (d_probs - inner_sum)
        scores_low = d_scores.astype(jnp.bfloat16)
        d_query = jnp.dot(scores_low, key_row, preferred_element_type=jnp.float32)
        d_key = lax.dot_general(
            scores_low, query_row, contract_rows, preferred_element_type=jnp.float32
        )
        d_value = lax.dot_general(
            attention.astype(jnp.bfloat16),
            grad_row,
            contract_rows,
            preferred_element_type=jnp.float32,
        )
        return (summed + d_scores, (d_query, d_key, d_value))

    tokens = bias_head.shape[1]
    return lax.scan(
        backward_one_row,
        jnp.zeros((tokens, tokens), jnp.float32),
        (query_h, key_h, value_h, grad_h),
    )


def body(
    pair, token_mask, chain_ids, proj_weight, bias_weight, chain_weight, out_weight, cotangent
):
    row_count, length, channels = pair.shape
    standard, inverse = normalize(pair)
    normed = standard.astype(jnp.bfloat16)
    flat_x = normed.reshape(row_count * length, channels)
    projected = jnp.dot(flat_x, proj_weight, preferred_element_type=jnp.float32).reshape(
        row_count, length, 4 * HD
    )
    scaling = DH ** (-0.5)
    query = (projected[..., :HD] * scaling).astype(jnp.bfloat16)
    key_rows = projected[..., HD : 2 * HD].astype(jnp.bfloat16)
    value_rows = projected[..., 2 * HD : 3 * HD].astype(jnp.bfloat16)
    gating = jax.nn.sigmoid(projected[..., 3 * HD :])
    local_bias = jnp.dot(flat_x, bias_weight, preferred_element_type=jnp.float32).reshape(
        row_count, length, H
    )
    local_bias = jnp.transpose(local_bias, (2, 0, 1)).astype(jnp.bfloat16)
    pair_bias = lax.all_gather(local_bias, "dap", axis=1, tiled=True)
    same_chain = (chain_ids[:, None] == chain_ids[None, :]).astype(jnp.float32)
    masked = (token_mask.astype(jnp.float32) - 1.0) * 1000000000.0
    outputs = []
    for number in range(H):
        columns = slice(number * DH, (number + 1) * DH)
        extra_head = chain_weight[number] * same_chain + masked[None, :]
        outputs.append(
            forward_rows(
                query[:, :, columns],
                key_rows[:, :, columns],
                value_rows[:, :, columns],
                pair_bias[number],
                extra_head,
            )
        )
    attended = jnp.concatenate(outputs, axis=-1)
    gated = (gating * attended).astype(jnp.bfloat16)
    gated_flat = gated.reshape(row_count * length, HD)
    update = jnp.dot(gated_flat, out_weight, preferred_element_type=jnp.float32).reshape(
        row_count, length, channels
    )
    next_pair = pair.astype(jnp.float32) + update
    next_pair_t = lax.all_to_all(
        jnp.transpose(next_pair, (1, 0, 2)), "dap", split_axis=0, concat_axis=1, tiled=True
    )
    grad_flat = cotangent.reshape(row_count * length, channels)
    out_part = (
        lax.dot_general(gated_flat, grad_flat, contract_rows, preferred_element_type=jnp.float32)
        / length
    )
    d_gated = lax.dot_general(
        grad_flat, out_weight, contract_cols, preferred_element_type=jnp.float32
    ).reshape(row_count, length, HD)
    d_attended = (d_gated * gating).astype(jnp.bfloat16)
    d_gate = d_gated * attended * gating * (1.0 - gating)
    query_parts, key_parts, value_parts, totals, shares = ([], [], [], [], [])
    for number in range(H):
        columns = slice(number * DH, (number + 1) * DH)
        extra_head = chain_weight[number] * same_chain + masked[None, :]
        summed, (d_query, d_key, d_value) = backward_rows(
            query[:, :, columns],
            key_rows[:, :, columns],
            value_rows[:, :, columns],
            d_attended[:, :, columns],
            pair_bias[number],
            extra_head,
        )
        query_parts.append(d_query)
        key_parts.append(d_key)
        value_parts.append(d_value)
        totals.append(summed)
    spread = lax.psum_scatter(jnp.stack(totals, axis=0), "dap", scatter_dimension=1, tiled=True)
    bias_total = jnp.transpose(spread, (1, 2, 0))
    d_proj = jnp.concatenate(
        [
            jnp.concatenate(query_parts, axis=-1) * scaling,
            jnp.concatenate(key_parts, axis=-1),
            jnp.concatenate(value_parts, axis=-1),
            d_gate,
        ],
        axis=-1,
    ).astype(jnp.bfloat16)
    d_bias = bias_total.astype(jnp.bfloat16)
    d_proj_flat = d_proj.reshape(row_count * length, 4 * HD)
    d_bias_flat = d_bias.reshape(row_count * length, H)
    d_normed = lax.dot_general(
        d_proj_flat, proj_weight, contract_cols, preferred_element_type=jnp.float32
    )
    d_normed = d_normed + lax.dot_general(
        d_bias_flat, bias_weight, contract_cols, preferred_element_type=jnp.float32
    )
    d_normed = d_normed.reshape(row_count, length, channels)
    mean_grad = jnp.mean(d_normed, axis=-1, keepdims=True)
    mean_cross = jnp.mean(d_normed * standard, axis=-1, keepdims=True)
    pair_grad = ((d_normed - mean_grad - standard * mean_cross) * inverse).astype(jnp.bfloat16)
    proj_part = (
        lax.dot_general(flat_x, d_proj_flat, contract_rows, preferred_element_type=jnp.float32)
        / length
    )
    biasw_part = (
        lax.dot_general(flat_x, d_bias_flat, contract_rows, preferred_element_type=jnp.float32)
        / length
    )
    start_row = lax.axis_index("dap") * row_count
    local_chain = lax.dynamic_slice_in_dim(chain_ids, start_row, row_count)
    same_local = (local_chain[:, None] == chain_ids[None, :]).astype(jnp.float32)
    chain_part = jnp.sum(bias_total * same_local[:, :, None], axis=(0, 1)) / length
    proj_grad, bias_weight_grad, chain_grad, out_grad = lax.psum(
        (proj_part, biasw_part, chain_part, out_part), "dap"
    )
    return (next_pair_t, pair_grad, proj_grad, bias_weight_grad, chain_grad, out_grad)


def solution(mesh):
    return jax.shard_map(
        body,
        mesh=mesh,
        in_specs=(
            P(("dp", "dap"), None, None),
            P("dp"),
            P("dp"),
            P(),
            P(),
            P(),
            P(),
            P(("dp", "dap"), None, None),
        ),
        out_specs=(
            P(("dp", "dap"), None, None),
            P(("dp", "dap"), None, None),
            P("dp", None),
            P("dp", None),
            P("dp"),
            P("dp", None),
        ),
        check_vma=False,
    )
```

profile of v0, /device:TPU:32, one launch (start us, length us, event | category | flops | bytes accessed | tf_op | source)
XLA Modules:
  0.0 1958.6 jit_solution(10141085470042809085)
XLA Ops:
  9.9 195.9 %all_gather.3 = bf16[4,256,256]{2,0,1:T(4,128)(2,1)S(1)} all-gather(bf16[4,2,256]{2,0,1:T(4,128)(2,1)S(1)} %fusion.179), channel_id=1, replica_groups=mesh['dap'=128,'dp'=2] {'dap'}, dimensions={1}, use_global_device_ids=true | all-gather | bytes 528384 | tf_op jit(solution)/shard_map/all_gather | solution.py:91
  211.1 5.6 while.115
  211.1 1.7 fusion.320
  213.9 1.7 fusion.320
  218.5 5.7 while.114
  218.5 1.8 fusion.316
  221.3 1.8 fusion.316
  226.0 3.6 while.113
  231.1 3.7 while.112
  231.1 1.6 fusion.308
  233.0 1.5 fusion.308
  236.3 1.9 multiply_convert_fusion
  239.4 6.2 all-to-all-start
  251.9 12.2 while.119
  264.9 8.8 while.118
  264.9 1.8 fusion.353
  269.3 1.8 fusion.353
  275.1 8.3 while.117
  275.1 1.6 fusion.341
  284.3 6.9 while.116
  287.7 1.6 fusion.329
  300.6 2.0 pad_maximum_fusion
  307.6 1290.5 %all-reduce.5.cloned.1.call-done = (f32[4,256,256]{2,0,1:T(4,128)}, f32[128,512]{1,0:T(8,128)}, f32[128,128]{1,0:T(8,128)}) async-done(((f32[4,256,256]{2,0,1:T(4,128)}, f32[128,512]{1,0:T(8,128)}, f32[128,128]{1,0:T(8,128)}), (f32[4,256,256]{2,0,1:T(4,128)}, f32[128,512]{1,0:T(8,128)}, f32[128,128]{1,0:T(8,128)})) %all-reduce.5.cloned.1.call-update) | async-done | bytes 1376272
  1602.4 347.9 %all-reduce.1 = (f32[128,4]{0,1:T(4,128)}, f32[4]{0:T(128)}) all-reduce(f32[128,4]{0,1:T(4,128)S(1)} %fusion.180, f32[4]{0:T(128)S(1)} %broadcast_multiply_fusion.3), channel_id=1, replica_groups=mesh['dap'=128,'dp'=2] {'dap'}, use_global_device_ids=true, to_apply=%region_42.43 | all-reduce | flops 516 | bytes 4128 | tf_op jit(solution)/shard_map/psum | solution.py:179
  (320 shorter events, 81.9 us)
Async XLA Ops:
  7.2 1.4 copy-start
  7.2 1.1 copy-start.1
  216.7 0.9 copy-start.4
  231.1 5.2 copy-start.41
  234.8 1.5 copy-start.56
  234.8 1.5 copy-start.14
  239.4 67.5 %all-to-all-start = ((f32[256,2,128]{2,1,0:T(2,128)}), f32[256,2,128]{2,1,0:T(2,128)S(1)}, u32[]{:S(2)}, u32[]{:S(2)}) async-start(f32[256,2,128]{2,1,0:T(2,128)} %copy.100), calls=%async_computation | async-start | bytes 524288 | tf_op jit(solution)/shard_map/all_to_all | solution.py:114
  245.6 1352.6 %all-reduce.5.cloned.1.call-start = ((), (), s32[]{:S(2)}) async-start(), calls=%async_computation.1 | async-start | bytes 2752512
  247.0 2.4 copy-start.42
  251.9 12.8 copy-start.3
  251.9 12.8 copy-start.23
  253.4 1.0 copy-start.48
  256.2 0.9 copy-start.49
  259.5 1.0 copy-start.48
  262.3 0.9 copy-start.49
  264.9 10.0 copy-start.19
  264.9 10.0 copy-start.25
  268.2 0.9 copy-start.47
  275.1 8.4 copy-start.17
  275.1 8.4 copy-start.21
  299.5 1.1 copy-start.5
  299.5 1.1 copy-start.6
  299.5 1.1 copy-start.7
  1601.4 348.9 %copy-start.15 = (f32[128,512]{1,0:T(8,128)S(1)}, f32[128,512]{1,0:T(8,128)}, u32[]{:S(2)}) copy-start(f32[128,512]{1,0:T(8,128)} %get-tuple-element.2116) | copy-start | bytes 786436
  (50 other events, 40.4 us)
Sparse Core Ops, SparseCore 0:
  302.8 1295.3 all-reduce.4
where the time goes:
time: 1960 us
  waiting for transfers between devices  1290 us (66%)
  blocking collectives  544 us (28%)
  local copies, waits for them, and re-layouts  51.2 us (3%)
  matrix products  40.6 us (2%)
    unnamed x2, waiting for transfers between devices  1290 us
    psum x1, blocking collectives, body(): lax.psum((proj_part, biasw_part, chain_part, out_part), 'dap')  348 us
    all_gather x1, blocking collectives, body(): pair_bias = lax.all_gather(local_bias, 'dap', axis=1, tiled=True)  196 us
  transfers between devices with their start and end apart: 2, of which 1 were waited for; matrix products, arithmetic and copies ran while one was open for 2% of the time, Pallas kernels for 0%

commit v1 on v0

--- a/solution.py
+++ b/solution.py
@@ -88,7 +88,9 @@
         row_count, length, H
     )
     local_bias = jnp.transpose(local_bias, (2, 0, 1)).astype(jnp.bfloat16)
-    pair_bias = lax.all_gather(local_bias, "dap", axis=1, tiled=True)
+    pair_bias = jnp.concatenate(
+        lax.all_to_all(jnp.stack(lax.axis_size("dap") * [local_bias], 0), "dap", 0, 0), 1
+    )
     same_chain = (chain_ids[:, None] == chain_ids[None, :]).astype(jnp.float32)
     masked = (token_mask.astype(jnp.float32) - 1.0) * 1000000000.0
     outputs = []

time: 1960 us -> 1820 us (0.929)
  blocking collectives: 544 us -> 348 us
  local copies, waits for them, and re-layouts: 51.2 us -> 77.5 us
    all_gather x1 -> x0, blocking collectives: 196 us -> none  [body(): pair_bias = lax.all_gather(local_bias, 'dap', axis=1, tiled=True)]
  transfers between devices with their start and end apart: 2 -> 3, of which waited for: 1 -> 2; matrix products, arithmetic and copies ran while one was open for 2% -> 3% of each run, Pallas kernels for 0% -> 0%
where the time goes in v1:
time: 1820 us; the launch traced here: 1810 us
  waiting for transfers between devices  1300 us (71%)
  blocking collectives  348 us (19%)
  local copies, waits for them, and re-layouts  77.5 us (4%)
  matrix products  45.6 us (3%)
  starting transfers between devices  21.3 us (1%)
    unnamed x2, waiting for transfers between devices  1290 us
    psum x1, blocking collectives, body(): lax.psum((proj_part, biasw_part, chain_part, out_part), 'dap')  348 us
  transfers between devices with their start and end apart: 3, of which 2 were waited for; matrix products, arithmetic and copies ran while one was open for 3% of the time, Pallas kernels for 0%

profile of v1, /device:TPU:32, one launch (start us, length us, event | category | flops | bytes accessed | tf_op | source)
XLA Modules:
  0.0 1814.9 jit_solution(2099227560655955000)
XLA Ops:
  10.6 14.9 all-to-all-start
  36.3 10.2 all-to-all-done
  49.5 7.0 while.115
  49.5 1.7 fusion.320
  53.0 1.7 fusion.320
  58.4 8.2 while.114
  59.0 1.8 fusion.316
  63.1 1.8 fusion.316
  68.5 8.1 while.113
  69.1 1.7 fusion.312
  73.1 1.7 fusion.312
  78.4 6.7 while.112
  79.0 1.8 fusion.308
  82.3 1.8 fusion.308
  85.9 2.2 multiply_convert_fusion
  90.8 6.2 all-to-all-start.1
  99.0 9.8 while.119
  110.5 10.7 while.118
  123.3 8.1 while.117
  133.3 12.9 while.116
  133.9 1.5 fusion.329
  158.0 2.0 pad_maximum_fusion
  167.7 1286.1 %all-reduce.5.cloned.1.call-done = (f32[4,256,256]{2,0,1:T(4,128)}, f32[128,512]{1,0:T(8,128)}, f32[128,128]{1,0:T(8,128)}) async-done(((f32[4,256,256]{2,0,1:T(4,128)}, f32[128,512]{1,0:T(8,128)}, f32[128,128]{1,0:T(8,128)}), (f32[4,256,256]{2,0,1:T(4,128)}, f32[128,512]{1,0:T(8,128)}, f32[128,128]{1,0:T(8,128)})) %all-reduce.5.cloned.1.call-update) | async-done | bytes 1376272
  1458.7 347.9 %all-reduce.1 = (f32[128,4]{0,1:T(4,128)}, f32[4]{0:T(128)}) all-reduce(f32[128,4]{0,1:T(4,128)S(1)} %fusion.180, f32[4]{0:T(128)S(1)} %broadcast_multiply_fusion.3), channel_id=1, replica_groups=mesh['dap'=128,'dp'=2] {'dap'}, use_global_device_ids=true, to_apply=%region_42.43 | all-reduce | flops 516 | bytes 4128 | tf_op jit(solution)/shard_map/psum | solution.py:181
  (387 shorter events, 114.5 us)
Async XLA Ops:
  7.2 27.3 %copy-start = (bf16[128,512]{1,0:T(8,128)(2,1)S(1)}, bf16[128,512]{1,0:T(8,128)(2,1)}, u32[]{:S(2)}) copy-start(bf16[128,512]{1,0:T(8,128)(2,1)} %param.27) | copy-start | bytes 393220
  7.2 1.1 copy-start.1
  10.6 35.9 %all-to-all-start = ((bf16[128,4,2,256]{3,2,1,0:T(2,128)(2,1)}), bf16[128,4,2,256]{3,2,1,0:T(2,128)(2,1)S(1)}, u32[]{:S(2)}, u32[]{:S(2)}) async-start(bf16[128,4,2,256]{3,2,1,0:T(2,128)(2,1)} %stack.12), calls=%async_computation | async-start | bytes 1048576 | tf_op jit(solution)/shard_map/all_to_all | solution.py:92
  48.6 1.0 copy-start.12
  57.4 1.0 copy-start.9
  67.6 1.0 copy-start.7
  90.8 76.1 %all-to-all-start.1 = ((f32[256,2,128]{2,1,0:T(2,128)}), f32[256,2,128]{2,1,0:T(2,128)S(1)}, u32[]{:S(2)}, u32[]{:S(2)}) async-start(f32[256,2,128]{2,1,0:T(2,128)} %copy.91), calls=%async_computation.1 | async-start | bytes 524288 | tf_op jit(solution)/shard_map/all_to_all | solution.py:116
  97.0 1356.7 %all-reduce.5.cloned.1.call-start = ((), (), s32[]{:S(2)}) async-start(), calls=%async_computation.2 | async-start | bytes 2752512
  97.2 0.9 copy-start.11
  97.2 1.0 copy-start.13
  97.3 1.1 copy-start.55
  102.9 0.9 copy-start.56
  107.8 0.9 copy-start.56
  109.6 0.9 copy-start.29
  121.2 1.3 copy-start.53
  121.8 0.9 copy-start.27
  131.3 1.3 copy-start.5
  131.3 1.3 copy-start.52
  131.9 1.0 copy-start.3
  154.4 1.0 copy-start.14
  154.4 1.0 copy-start.15
  156.9 1.1 copy-start.16
  156.9 1.1 copy-start.17
  1457.6 348.9 %copy-start.21 = (f32[128,512]{1,0:T(8,128)S(1)}, f32[128,512]{1,0:T(8,128)}, u32[]{:S(2)}) copy-start(f32[128,512]{1,0:T(8,128)} %get-tuple-element.2028) | copy-start | bytes 786436
  (81 other events, 62.3 us)
Sparse Core Ops, SparseCore 0:
  160.2 1293.5 all-reduce.4
